TPU v7x, 512 devices: a whole 4x4x16 slice. The times are simulated.
512 devices in a mesh: req: 64 (over x, z), tp: 8 (over y, core).
Axes of the slice: x: 4, y: 4, z: 16, core: 2. Of those that a mesh axis runs over, the one named last changes fastest.
Arguments:
- query_new: bfloat16 [8192, 2048], P('req', 'tp'), may hold values from -6 to 6
- key_new: bfloat16 [8192, 2048], P('req', 'tp'), may hold values from -6 to 6
- value_new: bfloat16 [8192, 2048], P('req', 'tp'), may hold values from -6 to 6
- mlp_hidden: bfloat16 [8192, 8192], P('req', 'tp'), may hold values from -6 to 6
- cache_pages: bfloat16 [4096, 16, 16, 256], P('req', None, 'tp'), may hold values from -6 to 6
- page_dest: int32 [4096, 1], P('req'), may hold values from 0 to 63; in each aligned block of 64 rows (0 to 63, 64 to 127, ...) at most 2 rows name the same one
- page_tag: int32 [4096], P('req'), may hold values from 0 to 3
- seg_ids: int32 [64, 128], P('req'), may hold values from 0 to 3, as said below
- attn_proj: bfloat16 [2048, 4096], P(('tp', 'req')), may hold values from -0.5 to 0.5
- mlp_down: bfloat16 [8192, 4096], P(('tp', 'req')), may hold values from -0.0625 to 0.0625
Outputs:
- layer_out: bfloat16 [8192, 4096], P('req', 'tp')
Inputs may be any that keep to these rules, and one draw needn't show every extreme that they name: `seg_ids`: within each pack the ids never fall; request 0 covers exactly the first 64 tokens and requests 1 to 3 each cover one or more of the rest. `page_dest`: among the rows of one device, at most 2 pages name the same destination, a bound that some block reaches.
All inputs are finite; a program needn't handle non-finite values.
Results may differ from a plain program's by a relative error of at most 0.014.
Values may be sent and summed in bfloat16 or wider, within the bound.
A program may use at most 128 MiB of HBM per device.

v0:
```python
import math
import jax
import jax.numpy as jnp
from jax import lax
from jax.sharding import PartitionSpec as P

HD = 128
ROT = 32
SEG_DEV = 4
CAP = 2


def rotate_heads(values, position, rot_dims):
    half_rot = rot_dims // 2
    frequency = 10000.0 ** (-2.0 * jnp.arange(half_rot, dtype=jnp.float32) / rot_dims)
    angles = position.astype(jnp.float32)[:, None] * frequency[None, :]
    cosine = jnp.cos(angles)[:, None, :]
    sine_part = jnp.sin(angles)[:, None, :]
    leading = values[..., :half_rot]
    trailing = values[..., half_rot:rot_dims]
    return jnp.concatenate(
        [
            leading * cosine - trailing * sine_part,
            trailing * cosine + leading * sine_part,
            values[..., rot_dims:],
        ],
        axis=-1,
    )


def masked_scores(query_rot, block_keys, segment, block_tags, score_scale):
    scores = (
        jnp.einsum("qhd,khd->hqk", query_rot, block_keys, preferred_element_type=jnp.float32)
        * score_scale
    )
    return jnp.where((segment[:, None] == block_tags[None, :])[None], scores, -jnp.inf)


def body(
    query_new,
    key_new,
    value_new,
    mlp_hidden,
    cache_pages,
    page_dest,
    page_tag,
    seg_ids,
    attn_proj,
    mlp_down,
):
    req_count = lax.axis_size("req")
    tok_count = query_new.shape[0]
    heads_local = query_new.shape[1] // HD
    page_rows = cache_pages.shape[1]
    pages_local = cache_pages.shape[0]
    slot_count = req_count * CAP
    score_scale = 1.0 / math.sqrt(HD)
    destination = page_dest[:, 0]
    dest_match = (destination[:, None] == jnp.arange(req_count, dtype=jnp.int32)[None, :]).astype(
        jnp.int32
    )
    earlier = jnp.cumsum(dest_match, axis=0) - dest_match
    rank = jnp.sum(earlier * dest_match, axis=1)
    slot_of_page = destination * CAP + rank
    select = jnp.arange(slot_count, dtype=jnp.int32)[:, None] == slot_of_page[None, :]
    flat_pages = cache_pages.reshape(pages_local, page_rows * heads_local * 2 * HD)
    send_pages = jnp.dot(
        select.astype(jnp.bfloat16), flat_pages, preferred_element_type=jnp.float32
    ).astype(jnp.bfloat16)
    send_pages = send_pages.reshape(req_count, CAP * page_rows, heads_local, 2 * HD)
    send_tags = (
        (jnp.sum(jnp.where(select, page_tag[None, :] + 1, 0), axis=1) - 1)
        .astype(jnp.bfloat16)
        .reshape(req_count, CAP)
    )
    recv_pages, recv_tags = (
        lax.all_to_all(send_pages, "req", split_axis=0, concat_axis=0, tiled=True),
        lax.all_to_all(send_tags, "req", split_axis=0, concat_axis=0, tiled=True),
    )
    slot_pages = recv_pages.reshape(slot_count, page_rows, heads_local, 2 * HD)
    slot_tags = recv_tags.reshape(slot_count).astype(jnp.int32)
    segment = seg_ids[0]
    seg_range = jnp.arange(SEG_DEV, dtype=jnp.int32)
    seg_first = jnp.sum((segment[:, None] < seg_range[None, :]).astype(jnp.int32), axis=0)
    prefix = page_rows * jnp.sum(
        (slot_tags[:, None] == seg_range[None, :]).astype(jnp.int32), axis=0
    )
    seg_match = segment[:, None] == seg_range[None, :]
    offset = jnp.sum(jnp.where(seg_match, prefix[None, :] - seg_first[None, :], 0), axis=1)
    row_index = jnp.arange(tok_count, dtype=jnp.int32)
    position = row_index + offset
    query_rot = rotate_heads(
        query_new.reshape(tok_count, heads_local, HD).astype(jnp.float32), position, ROT
    ).astype(jnp.bfloat16)
    key_rot = rotate_heads(
        key_new.reshape(tok_count, heads_local, HD).astype(jnp.float32), position, ROT
    ).astype(jnp.bfloat16)
    value_heads = value_new.reshape(tok_count, heads_local, HD)
    local_scores = (
        jnp.einsum("qhd,khd->hqk", query_rot, key_rot, preferred_element_type=jnp.float32)
        * score_scale
    )
    causal = (segment[:, None] == segment[None, :]) & (row_index[None, :] <= row_index[:, None])
    local_scores = jnp.where(causal[None], local_scores, -jnp.inf)
    cache_rows = slot_pages.reshape(slot_count * page_rows, heads_local, 2 * HD)
    key_tags = jnp.repeat(slot_tags, page_rows)
    cached = masked_scores(query_rot, cache_rows[..., :HD], segment, key_tags, score_scale)
    row_max = jnp.maximum(jnp.max(local_scores, axis=2), jnp.max(cached, axis=2))
    local_exp = jnp.exp(local_scores - row_max[..., None])
    cached_exp = jnp.exp(cached - row_max[..., None])
    denominator = jnp.sum(local_exp, axis=2) + jnp.sum(cached_exp, axis=2)
    local_weights = (local_exp / denominator[..., None]).astype(jnp.bfloat16)
    cached_weights = (cached_exp / denominator[..., None]).astype(jnp.bfloat16)
    attention = jnp.einsum(
        "hqk,khd->qhd", local_weights, value_heads, preferred_element_type=jnp.float32
    )
    attention = attention + jnp.einsum(
        "hqk,khd->qhd", cached_weights, cache_rows[..., HD:], preferred_element_type=jnp.float32
    )
    attn_flat = attention.astype(jnp.bfloat16).reshape(tok_count, heads_local * HD)
    columns = attn_flat
    attn_part = jnp.dot(
        columns,
        lax.all_gather(attn_proj, "req", axis=0, tiled=True),
        preferred_element_type=jnp.float32,
    )
    columns = mlp_hidden
    partial_value = attn_part + jnp.dot(
        columns,
        lax.all_gather(mlp_down, "req", axis=0, tiled=True),
        preferred_element_type=jnp.float32,
    )
    return lax.psum_scatter(
        partial_value.astype(jnp.bfloat16), "tp", scatter_dimension=1, tiled=True
    )


def solution(mesh):
    return jax.shard_map(
        body,
        mesh=mesh,
        in_specs=(
            P("req", "tp"),
            P("req", "tp"),
            P("req", "tp"),
            P("req", "tp"),
            P("req", None, "tp", None),
            P("req", None),
            P("req"),
            P("req", None),
            P(("tp", "req"), None),
            P(("tp", "req"), None),
        ),
        out_specs=P("req", "tp"),
        check_vma=False,
    )
```

profile of v0, /device:TPU:4, one launch (start us, length us, event | category | flops | bytes accessed | tf_op | source)
XLA Modules:
  0.0 378.9 jit_solution(5007309284389272083)
XLA Ops:
  6.5 0.0 copy-start
  6.5 0.0 all-gather.6.cloned.1.call-start
  6.5 0.7 all-gather.6.cloned.1.call-update
  7.3 0.0 all-gather.4.cloned.1.call-start
  7.3 0.7 all-gather.4.cloned.1.call-update
  8.0 0.7 fusion.17
  8.7 0.1 reduce_window_sum.11
  8.8 0.8 select_reduce_fusion.1
  9.7 0.7 multiply_add_fusion
  10.4 0.1 select_reduce_fusion
  10.5 0.8 convert_element_type.89
  11.3 18.7 %all-to-all-start = ((bf16[64,1,2]{2,1,0:T(2,128)(2,1)}), bf16[64,1,2]{2,1,0:T(2,128)(2,1)S(1)}, u32[]{:S(2)}, u32[]{:S(2)}) async-start(bf16[64,1,2]{2,1,0:T(2,128)(2,1)} %convert_element_type.89), calls=%async_computation | async-start | bytes 65536 | tf_op jit(solution)/shard_map/all_to_all | solution.py:78
  30.0 1.8 reshape.208
  31.8 0.8 convolution_convert_fusion
  32.6 2.8 reshape.209
  35.4 0.0 copy-start.2
  35.5 0.0 copy-start.3
  35.5 0.0 copy-start.4
  35.5 0.0 copy-start.5
  35.5 7.2 %all-to-all-done = bf16[64,1,2]{2,1,0:T(2,128)(2,1)S(1)} async-done(((bf16[64,1,2]{2,1,0:T(2,128)(2,1)}), bf16[64,1,2]{2,1,0:T(2,128)(2,1)S(1)}, u32[]{:S(2)}, u32[]{:S(2)}) %all-to-all-start) | async-done | bytes 288 | tf_op jit(solution)/shard_map/all_to_all | solution.py:78
  42.6 8.1 %all-to-all-start.1 = ((bf16[64,32,2,256]{3,2,1,0:T(2,128)(2,1)}), bf16[64,32,2,256]{3,2,1,0:T(2,128)(2,1)S(1)}, u32[]{:S(2)}, u32[]{:S(2)}) async-start(bf16[64,32,2,256]{3,2,1,0:T(2,128)(2,1)} %reshape.209), calls=%async_computation.1 | async-start | bytes 4194304 | tf_op jit(solution)/shard_map/all_to_all | solution.py:77
  50.8 0.0 reduce-scatter.2.cloned.1.call-start
  50.8 0.0 copy-done.2
  50.8 0.1 copy.47
  50.9 0.1 copy.48
  51.1 0.1 slice.36
  51.2 0.0 copy-done.3
  51.2 0.1 copy.53
  51.3 0.1 copy.54
  51.5 0.1 slice.39
  51.5 0.0 copy-done.4
  51.6 0.1 copy.62
  51.7 0.0 copy-done.5
  51.7 0.1 convert_reduce_fusion.1
  51.8 0.1 fusion.16
  51.9 0.1 convert_reduce_fusion
  52.0 0.1 reshape.212
  52.2 0.1 convert_reduce_fusion.2
  52.3 0.1 select_reduce_fusion.2
  52.4 0.1 multiply_cosine_fusion
  52.5 0.1 copy.51
  52.6 0.1 copy.50
  52.7 0.1 broadcast_in_dim.56
  52.8 0.1 eq.110
  52.9 0.1 subtract_convert_fusion
  53.0 0.3 fusion.20
  53.3 0.2 broadcast_compare_fusion
  53.5 121.6 %all-gather.6.cloned.1.call-done = bf16[64,4,4096]{2,1,0:T(4,128)(2,1)} async-done(((bf16[1,4,4096]{2,1,0:T(4,128)(2,1)}), bf16[64,4,4096]{2,1,0:T(4,128)(2,1)}) %all-gather.6.cloned.1.call-update) | async-done | bytes 2097168 | tf_op jit(solution)/shard_map/all_gather | solution.py:124
  175.1 4.0 %reshape.214 = bf16[256,4096]{1,0:T(8,128)(2,1)} reshape(bf16[64,4,4096]{2,1,0:T(4,128)(2,1)} %all-gather.6.cloned.1.call-done) | data formatting | bytes 4194304
  179.1 0.0 all-to-all-done.1
  179.1 0.4 copy.56
  179.6 0.7 fusion.21
  180.4 0.4 fusion.2
  180.8 0.8 convolution_bitcast_fusion.1
  181.6 0.2 fusion.5
  181.8 0.0 copy-start.1
  181.8 147.8 %all-gather.4.cloned.1.call-done = bf16[1024,4096]{1,0:T(8,128)(2,1)} async-done(((bf16[16,4096]{1,0:T(8,128)(2,1)}), bf16[1024,4096]{1,0:T(8,128)(2,1)}) %all-gather.4.cloned.1.call-update) | async-done | bytes 8388624 | tf_op jit(solution)/shard_map/all_gather | solution.py:130
  329.6 0.0 copy-done
  329.6 4.6 %fusion.22 = f32[128,4096]{1,0:T(8,128)S(1)} fusion(bf16[128,1024]{1,0:T(8,128)(2,1)S(1)} %copy-done, bf16[1024,4096]{1,0:T(8,128)(2,1)} %all-gather.4.cloned.1.call-done), kind=kOutput, calls=%fused_computation.58 | convolution fusion | flops 1073741824 | bytes 10747904 | tf_op jit(solution)/shard_map/dot_general | solution.py:128
  334.2 0.0 copy-done.1
  334.2 1.5 fusion
  335.7 0.0 reduce-scatter.2.cloned.1.call-update
  335.8 36.6 %reduce-scatter.2.cloned.1.call-done = bf16[128,512]{1,0:T(8,128)(2,1)} async-done(((bf16[128,4096]{1,0:T(8,128)(2,1)}), bf16[128,512]{1,0:T(8,128)(2,1)}) %reduce-scatter.2.cloned.1.call-update) | async-done | bytes 131088 | tf_op jit(solution)/shard_map/reduce_scatter | solution.py:133
  (9 shorter events, 0.1 us)
Async XLA Ops:
  6.5 323.0 %copy-start = (bf16[128,1024]{1,0:T(8,128)(2,1)S(1)}, bf16[128,1024]{1,0:T(8,128)(2,1)}, u32[]{:S(2)}) copy-start(bf16[128,1024]{1,0:T(8,128)(2,1)} %param.13) | copy-start | bytes 786436
  6.5 168.6 %all-gather.6.cloned.1.call-start = ((), (), s32[]{:S(2)}) async-start(), calls=%async_computation.5 | async-start | bytes 2129920 | tf_op jit(solution)/shard_map/all_gather | solution.py:124
  7.3 322.3 %all-gather.4.cloned.1.call-start = ((), (), s32[]{:S(2)}) async-start(), calls=%async_computation.3 | async-start | bytes 8519680 | tf_op jit(solution)/shard_map/all_gather | solution.py:130
  11.3 31.4 %all-to-all-start = ((bf16[64,1,2]{2,1,0:T(2,128)(2,1)}), bf16[64,1,2]{2,1,0:T(2,128)(2,1)S(1)}, u32[]{:S(2)}, u32[]{:S(2)}) async-start(bf16[64,1,2]{2,1,0:T(2,128)(2,1)} %convert_element_type.89), calls=%async_computation | async-start | bytes 65536 | tf_op jit(solution)/shard_map/all_to_all | solution.py:78
  35.4 15.4 %copy-start.2 = (bf16[128,256]{1,0:T(8,128)(2,1)S(1)}, bf16[128,256]{1,0:T(8,128)(2,1)}, u32[]{:S(2)}) copy-start(bf16[128,256]{1,0:T(8,128)(2,1)} %param.10) | copy-start | bytes 196612
  35.5 15.7 %copy-start.3 = (bf16[128,256]{1,0:T(8,128)(2,1)S(1)}, bf16[128,256]{1,0:T(8,128)(2,1)}, u32[]{:S(2)}) copy-start(bf16[128,256]{1,0:T(8,128)(2,1)} %param.11) | copy-start | bytes 196612
  35.5 16.1 %copy-start.4 = (bf16[128,256]{1,0:T(8,128)(2,1)S(1)}, bf16[128,256]{1,0:T(8,128)(2,1)}, u32[]{:S(2)}) copy-start(bf16[128,256]{1,0:T(8,128)(2,1)} %param.12) | copy-start | bytes 196612
  35.5 16.2 %copy-start.5 = (s32[1,128]{1,0:T(1,128)S(1)}, s32[1,128]{1,0:T(1,128)}, u32[]{:S(2)}) copy-start(s32[1,128]{1,0:T(1,128)} %param.17) | copy-start | bytes 1540
  42.6 136.5 %all-to-all-start.1 = ((bf16[64,32,2,256]{3,2,1,0:T(2,128)(2,1)}), bf16[64,32,2,256]{3,2,1,0:T(2,128)(2,1)S(1)}, u32[]{:S(2)}, u32[]{:S(2)}) async-start(bf16[64,32,2,256]{3,2,1,0:T(2,128)(2,1)} %reshape.209), calls=%async_computation.1 | async-start | bytes 4194304 | tf_op jit(solution)/shard_map/all_to_all | solution.py:77
  50.8 321.7 %reduce-scatter.2.cloned.1.call-start = ((), (), s32[]{:S(2)}) async-start(), calls=%async_computation.4 | async-start | bytes 1179648 | tf_op jit(solution)/shard_map/reduce_scatter | solution.py:133
  181.8 152.4 %copy-start.1 = (bf16[256,4096]{1,0:T(8,128)(2,1)S(1)}, bf16[256,4096]{1,0:T(8,128)(2,1)}, u32[]{:S(2)}) copy-start(bf16[256,4096]{1,0:T(8,128)(2,1)} %reshape.214) | copy-start | bytes 6291460
Sparse Core Ops, SparseCore 0:
  10.3 164.8 all-gather.5
  178.1 151.4 all-gather.3
  335.9 36.4 reduce-scatter.1
where the time goes:
time: 379 us
  waiting for transfers between devices  315 us (83%)
  starting transfers between devices  26.9 us (7%)
  between operations  13.3 us (4%)
  local copies, waits for them, and re-layouts  11.2 us (3%)
  matrix products  8.96 us (2%)
  other arithmetic  3.99 us (1%)
    all_gather x1, waiting for transfers between devices, body(): lax.all_gather(mlp_down, 'req', axis=0, tiled=True)  148 us
    all_gather x1, waiting for transfers between devices, body(): lax.all_gather(attn_proj, 'req', axis=0, tiled=True)  122 us
    reduce_scatter x1, waiting for transfers between devices, body(): lax.psum_scatter(partial_value.astype(jnp.bfloat16), 'tp', scatter_dimens...  36.6 us
    all_to_all x1, starting transfers between devices, body(): lax.all_to_all(send_tags, 'req', split_axis=0, concat_axis=0, tiled=True)  18.7 us
    all_to_all x1, starting transfers between devices, body(): lax.all_to_all(send_pages, 'req', split_axis=0, concat_axis=0, tiled=True)  8.11 us
  transfers between devices with their start and end apart: 5, of which 4 were waited for; matrix products, arithmetic and copies ran while one was open for 5% of the time, Pallas kernels for 0%

commit v1 on v0

--- a/solution.py
+++ b/solution.py
@@ -127,7 +127,9 @@
     columns = mlp_hidden
     partial_value = attn_part + jnp.dot(
         columns,
-        lax.all_gather(mlp_down, "req", axis=0, tiled=True),
+        jnp.concatenate(
+            lax.all_to_all(jnp.stack([mlp_down] * lax.axis_size("req")), "req", 0, 0), axis=0
+        ),
         preferred_element_type=jnp.float32,
     )
     return lax.psum_scatter(

time: 379 us -> 587 us (1.55)
  the two profiles are of different devices: /device:TPU:4 before, /device:TPU:6 now
where the time goes in v1:
time: 587 us; the launch traced here: 586 us
  waiting for transfers between devices  412 us (70%)
  blocking collectives  106 us (18%)
  starting transfers between devices  26.5 us (5%)
  local copies, waits for them, and re-layouts  15.4 us (3%)
  between operations  13.6 us (2%)
  matrix products  9.06 us (2%)
    all_gather x1, waiting for transfers between devices, body(): lax.all_gather(attn_proj, 'req', axis=0, tiled=True)  197 us
    all_to_all x1, waiting for transfers between devices, body(): lax.all_to_all(jnp.stack([mlp_down] * lax.axis_size('req')), 'req', 0, 0)  171 us
    all_to_all x1, blocking collectives, body(): lax.all_to_all(send_pages, 'req', split_axis=0, concat_axis=0, tiled=True)  106 us
    reduce_scatter x1, waiting for transfers between devices, body(): lax.psum_scatter(partial_value.astype(jnp.bfloat16), 'tp', scatter_dimens...  35.9 us
    all_to_all x1, starting transfers between devices, body(): lax.all_to_all(send_tags, 'req', split_axis=0, concat_axis=0, tiled=True)  18.8 us
  transfers between devices with their start and end apart: 4, of which 4 were waited for; matrix products, arithmetic and copies ran while one was open for 2% of the time, Pallas kernels for 0%

profile of v1, /device:TPU:6, one launch (start us, length us, event | category | flops | bytes accessed | tf_op | source)
XLA Modules:
  0.0 586.1 jit_solution(15640518928090655160)
XLA Ops:
  6.5 0.0 copy-start
  6.5 0.8 fusion.17
  7.3 0.1 reduce_window_sum.11
  7.4 0.8 select_reduce_fusion.1
  8.2 0.7 multiply_add_fusion
  8.9 0.1 select_reduce_fusion
  9.0 0.8 convert_element_type.89
  9.8 18.8 %all-to-all-start = ((bf16[64,1,2]{2,1,0:T(2,128)(2,1)}), bf16[64,1,2]{2,1,0:T(2,128)(2,1)S(1)}, u32[]{:S(2)}, u32[]{:S(2)}) async-start(bf16[64,1,2]{2,1,0:T(2,128)(2,1)} %convert_element_type.89), calls=%async_computation | async-start | bytes 65536 | tf_op jit(solution)/shard_map/all_to_all | solution.py:78
  28.6 1.8 reshape.213
  30.5 0.8 convolution_convert_fusion
  31.3 2.8 reshape.214
  34.1 0.0 copy-start.2
  34.1 7.1 %all-to-all-done = bf16[64,1,2]{2,1,0:T(2,128)(2,1)S(1)} async-done(((bf16[64,1,2]{2,1,0:T(2,128)(2,1)}), bf16[64,1,2]{2,1,0:T(2,128)(2,1)S(1)}, u32[]{:S(2)}, u32[]{:S(2)}) %all-to-all-start) | async-done | bytes 288 | tf_op jit(solution)/shard_map/all_to_all | solution.py:78
  41.1 105.9 %all_to_all.16 = bf16[64,32,2,256]{3,2,1,0:T(2,128)(2,1)S(1)} all-to-all(bf16[64,32,2,256]{3,2,1,0:T(2,128)(2,1)} %reshape.214), channel_id=1, replica_groups=mesh['req'=64,'tp'=8] {'req'}, dimensions={0} | all-to-all | bytes 4194304 | tf_op jit(solution)/shard_map/all_to_all | solution.py:77
  147.0 0.0 copy-done.2
  147.0 4.3 stack.2
  151.3 0.0 copy-start.3
  151.3 0.0 copy-start.4
  151.3 0.0 copy-start.5
  151.3 0.0 copy-start.6
  151.3 7.7 %all-to-all-start.2 = ((bf16[64,16,4096]{2,1,0:T(8,128)(2,1)}), bf16[64,16,4096]{2,1,0:T(8,128)(2,1)}, u32[]{:S(2)}, u32[]{:S(2)}) async-start(bf16[64,16,4096]{2,1,0:T(8,128)(2,1)} %stack.2), calls=%async_computation.2 | async-start | bytes 16777216 | tf_op jit(solution)/shard_map/all_to_all | solution.py:131
  159.0 0.0 all-gather.3.cloned.1.call-start
  159.0 0.7 all-gather.3.cloned.1.call-update
  159.7 0.0 reduce-scatter.2.cloned.1.call-start
  159.8 0.0 copy-done.3
  159.8 0.1 copy.47
  159.9 0.1 copy.48
  160.0 0.1 slice.36
  160.2 0.0 copy-done.4
  160.2 0.1 copy.53
  160.3 0.1 copy.54
  160.4 0.1 slice.39
  160.5 0.0 copy-done.5
  160.5 0.1 copy.62
  160.7 0.0 copy-done.6
  160.7 0.1 convert_reduce_fusion.1
  160.8 0.1 fusion.16
  160.9 0.1 convert_reduce_fusion
  161.0 0.1 reshape.218
  161.1 0.1 convert_reduce_fusion.2
  161.3 0.1 select_reduce_fusion.2
  161.4 0.1 multiply_cosine_fusion
  161.5 0.1 copy.51
  161.6 0.1 copy.50
  161.7 0.1 broadcast_in_dim.56
  161.8 0.1 eq.110
  161.9 0.1 subtract_convert_fusion
  162.0 0.3 fusion.20
  162.3 0.2 broadcast_compare_fusion
  162.5 197.2 %all-gather.3.cloned.1.call-done = bf16[64,4,4096]{2,1,0:T(4,128)(2,1)} async-done(((bf16[1,4,4096]{2,1,0:T(4,128)(2,1)}), bf16[64,4,4096]{2,1,0:T(4,128)(2,1)}) %all-gather.3.cloned.1.call-update) | async-done | bytes 2097168 | tf_op jit(solution)/shard_map/all_gather | solution.py:124
  359.8 4.0 reshape.220
  363.7 0.4 copy.56
  364.2 0.7 fusion.21
  365.0 0.4 fusion.2
  365.4 0.8 convolution_bitcast_fusion.1
  366.2 0.2 fusion.5
  366.4 170.7 %all-to-all-done.2 = bf16[64,16,4096]{2,1,0:T(8,128)(2,1)} async-done(((bf16[64,16,4096]{2,1,0:T(8,128)(2,1)}), bf16[64,16,4096]{2,1,0:T(8,128)(2,1)}, u32[]{:S(2)}, u32[]{:S(2)}) %all-to-all-start.2) | async-done | bytes 8388640 | tf_op jit(solution)/shard_map/all_to_all | solution.py:131
  537.1 0.0 copy-done
  537.1 0.0 copy-start.1
  537.1 4.8 fusion.22
  541.9 0.0 copy-done.1
  541.9 1.5 fusion
  543.4 0.0 reduce-scatter.2.cloned.1.call-update
  543.4 35.9 %reduce-scatter.2.cloned.1.call-done = bf16[128,512]{1,0:T(8,128)(2,1)} async-done(((bf16[128,4096]{1,0:T(8,128)(2,1)}), bf16[128,512]{1,0:T(8,128)(2,1)}) %reduce-scatter.2.cloned.1.call-update) | async-done | bytes 131088 | tf_op jit(solution)/shard_map/reduce_scatter | solution.py:135
  (9 shorter events, 0.1 us)
Async XLA Ops:
  6.5 530.6 %copy-start = (bf16[128,1024]{1,0:T(8,128)(2,1)S(1)}, bf16[128,1024]{1,0:T(8,128)(2,1)}, u32[]{:S(2)}) copy-start(bf16[128,1024]{1,0:T(8,128)(2,1)} %param.13) | copy-start | bytes 786436
  9.8 31.3 %all-to-all-start = ((bf16[64,1,2]{2,1,0:T(2,128)(2,1)}), bf16[64,1,2]{2,1,0:T(2,128)(2,1)S(1)}, u32[]{:S(2)}, u32[]{:S(2)}) async-start(bf16[64,1,2]{2,1,0:T(2,128)(2,1)} %convert_element_type.89), calls=%async_computation | async-start | bytes 65536 | tf_op jit(solution)/shard_map/all_to_all | solution.py:78
  34.1 113.0 %copy-start.2 = (bf16[16,4096]{1,0:T(8,128)(2,1)S(1)}, bf16[16,4096]{1,0:T(8,128)(2,1)}, u32[]{:S(2)}) copy-start(bf16[16,4096]{1,0:T(8,128)(2,1)} %param.19) | copy-start | bytes 393220
  151.3 8.5 %copy-start.3 = (bf16[128,256]{1,0:T(8,128)(2,1)S(1)}, bf16[128,256]{1,0:T(8,128)(2,1)}, u32[]{:S(2)}) copy-start(bf16[128,256]{1,0:T(8,128)(2,1)} %param.10) | copy-start | bytes 196612
  151.3 8.9 %copy-start.4 = (bf16[128,256]{1,0:T(8,128)(2,1)S(1)}, bf16[128,256]{1,0:T(8,128)(2,1)}, u32[]{:S(2)}) copy-start(bf16[128,256]{1,0:T(8,128)(2,1)} %param.11) | copy-start | bytes 196612
  151.3 9.2 %copy-start.5 = (bf16[128,256]{1,0:T(8,128)(2,1)S(1)}, bf16[128,256]{1,0:T(8,128)(2,1)}, u32[]{:S(2)}) copy-start(bf16[128,256]{1,0:T(8,128)(2,1)} %param.12) | copy-start | bytes 196612
  151.3 9.4 %copy-start.6 = (s32[1,128]{1,0:T(1,128)S(1)}, s32[1,128]{1,0:T(1,128)}, u32[]{:S(2)}) copy-start(s32[1,128]{1,0:T(1,128)} %param.17) | copy-start | bytes 1540
  151.3 385.8 %all-to-all-start.2 = ((bf16[64,16,4096]{2,1,0:T(8,128)(2,1)}), bf16[64,16,4096]{2,1,0:T(8,128)(2,1)}, u32[]{:S(2)}, u32[]{:S(2)}) async-start(bf16[64,16,4096]{2,1,0:T(8,128)(2,1)} %stack.2), calls=%async_computation.2 | async-start | bytes 16777216 | tf_op jit(solution)/shard_map/all_to_all | solution.py:131
  159.0 200.8 %all-gather.3.cloned.1.call-start = ((), (), s32[]{:S(2)}) async-start(), calls=%async_computation.5 | async-start | bytes 2129920 | tf_op jit(solution)/shard_map/all_gather | solution.py:124
  159.7 419.6 %reduce-scatter.2.cloned.1.call-start = ((), (), s32[]{:S(2)}) async-start(), calls=%async_computation.4 | async-start | bytes 1179648 | tf_op jit(solution)/shard_map/reduce_scatter | solution.py:135
  537.1 4.8 copy-start.1
Sparse Core Ops, SparseCore 0:
  162.8 196.9 all-gather.2
  543.5 35.7 reduce-scatter.1
